TPU v7x, 256 devices: a whole 4x4x8 slice. The times are simulated.
256 devices in a mesh: space: 32 (over y, z_hi, core), test: 2 (over z_lo), trial: 4 (over x).
Axes of the slice: x: 4, y: 4, z: 8 (z_hi: 4, z_lo: 2; z = z_hi * 2 + z_lo), core: 2. Of those that a mesh axis runs over, the one named last changes fastest.
Arguments:
- test_modes: bfloat16 [3, 128, 128, 8, 128], P(None, 'test', 'space'), may hold values from -6 to 6
- trial_modes: bfloat16 [3, 128, 128, 8, 128], P(None, 'trial', 'space'), may hold values from -6 to 6
- volumes: float32 [128, 8, 128], P('space'), may hold values from 0.25 to 4
Outputs:
- tensor: float32 [128, 128, 128], P('space', 'test', 'trial')
All inputs are finite; a program needn't handle non-finite values.
Results may differ from a plain program's by a relative error of at most 0.0051.
Values may be sent and summed in bfloat16 or wider, within the bound.
No kernel may reach another device: no remote copies, remote signals or barrier semaphores. Data moves between devices by JAX's collectives and lax.ppermute only.
A program may use at most 64 MiB of HBM per device.

v0:
```python
import math

import jax
import jax.numpy as jnp
from jax import lax
from jax.sharding import PartitionSpec as P


def with_halo(cells, sides, width):
    for axis, dim in sides:
        count = lax.axis_size(axis)
        ends = count - 1
        head = lax.slice_in_dim(cells, 0, width, axis=dim)
        tail = lax.slice_in_dim(cells, cells.shape[dim] - width, cells.shape[dim], axis=dim)
        cells = jnp.concatenate(
            [
                lax.ppermute(tail, axis, [(i, (i + 1) % count) for i in range(ends)]),
                cells,
                lax.ppermute(head, axis, [((i + 1) % count, i) for i in range(ends)]),
            ],
            axis=dim,
        )
    return cells


def derivatives(padded):
    field = padded.astype(jnp.float32)
    along_x = (field[:, :, 2:] - field[:, :, :-2]) * 0.5
    center = field[:, :, 1:-1]
    wide_y = jnp.pad(center, ((0, 0), (0, 0), (0, 0), (1, 1), (0, 0)))
    along_y = (wide_y[:, :, :, 2:] - wide_y[:, :, :, :-2]) * 0.5
    wide_z = jnp.pad(center, ((0, 0), (0, 0), (0, 0), (0, 0), (1, 1)))
    along_z = (wide_z[:, :, :, :, 2:] - wide_z[:, :, :, :, :-2]) * 0.5
    return jnp.stack([along_x, along_y, along_z], axis=1).astype(jnp.bfloat16)


def pick_row(array, plane, row, first):
    return lax.dynamic_index_in_dim(
        lax.dynamic_index_in_dim(array, plane, first, False), row, first, False
    )


def block_terms(mode_rows, grad_rows, weighted):
    width_j = mode_rows.shape[1]
    width_k = grad_rows.shape[2]
    planes = mode_rows.shape[2]
    rows_each = mode_rows.shape[3]

    def advance(position, running):
        plane = position // rows_each
        row = position % rows_each
        trial_block = pick_row(mode_rows, plane, row, 2)
        grad_block = pick_row(grad_rows, plane, row, 3)
        test_block = pick_row(weighted, plane, row, 2)
        convected = jnp.einsum(
            "bjc,abkc->ajkc", trial_block, grad_block, preferred_element_type=jnp.float32
        ).astype(jnp.bfloat16)
        return running + jnp.einsum(
            "aic,ajkc->jik", test_block, convected, preferred_element_type=jnp.float32
        )

    running = jnp.zeros((width_j, weighted.shape[1], width_k), jnp.float32)
    return lax.fori_loop(0, planes * rows_each, advance, running)


def finish(partial_value, factor):
    return lax.psum_scatter(partial_value, "space", scatter_dimension=0, tiled=True) * factor


def shards(test_modes, trial_modes, volumes):
    cell_count = trial_modes.shape[2] * trial_modes.shape[3] * trial_modes.shape[4]
    factor = 1.0 / (4.0 * math.sqrt(cell_count * lax.axis_size("space")))
    padded = with_halo(trial_modes, (("space", 2),), 1)
    gradients = derivatives(padded)
    weighted = (test_modes.astype(jnp.float32) * volumes).astype(jnp.bfloat16)
    all_modes = lax.all_gather(trial_modes, "trial", axis=1, tiled=True)
    partial_value = block_terms(all_modes, gradients, weighted)
    return finish(partial_value, factor)


def solution(mesh):
    return jax.shard_map(
        shards,
        mesh=mesh,
        in_specs=(
            P(None, "test", "space", None, None),
            P(None, "trial", "space", None, None),
            P("space", None, None),
        ),
        out_specs=P("space", "test", "trial"),
        check_vma=False,
    )
```

profile of v0, /device:TPU:2, one launch (start us, length us, event | category | flops | bytes accessed | tf_op | source)
XLA Modules:
  0.0 535.8 jit_solution(14520357436832206297)
XLA Ops:
  21.6 31.8 %all-gather.2.cloned.1.call-done = bf16[3,128,4,8,128]{4,1,0,3,2:T(8,128)(2,1)} async-done(((bf16[3,32,4,8,128]{4,1,0,3,2:T(8,128)(2,1)}), bf16[3,128,4,8,128]{4,1,0,3,2:T(8,128)(2,1)}) %all-gather.2.cloned.1.call-update) | async-done | bytes 3145744 | tf_op jit(solution)/shard_map/all_gather | solution.py:76
  53.4 376.8 %while.17 = (s32[]{:T(128)}, f32[128,64,32]{0,1,2:T(8,128)}, bf16[3,3,32,4,8,128]{5,2,1,0,4,3:T(8,128)(2,1)}, bf16[3,128,4,8,128]{4,1,0,3,2:T(8,128)(2,1)}, bf16...) while((s32[]{:T(128)}, f32[128,64,32]{0,1,2:T(8,128)}, ...), condition=%wide.region_1.2_spmd.clone, body=%wide.region_0.1_spmd.clone.sunk | while | flops 211288080 | bytes 15589742 | solution.py:63
  58.0 3.8 copy.26
  81.1 3.8 copy.26
  92.9 3.8 copy.26
  104.7 3.8 copy.26
  116.5 3.8 copy.26
  128.3 3.8 copy.26
  140.1 3.8 copy.26
  151.9 3.8 copy.26
  163.7 3.8 copy.26
  175.5 3.8 copy.26
  187.3 3.8 copy.26
  199.0 3.8 copy.26
  210.8 3.8 copy.26
  222.6 3.8 copy.26
  234.4 3.8 copy.26
  246.2 3.8 copy.26
  269.8 3.8 copy.26
  281.6 3.8 copy.26
  305.1 3.8 copy.26
  316.9 3.8 copy.26
  328.7 3.8 copy.26
  340.5 3.8 copy.26
  352.3 3.8 copy.26
  364.1 3.8 copy.26
  375.9 3.8 copy.26
  387.7 3.8 copy.26
  399.5 3.8 copy.26
  411.3 3.8 copy.26
  430.2 4.0 copy.15
  434.2 93.2 %reduce-scatter.2.cloned.1.call-done = f32[4,64,32]{1,2,0:T(8,128)} async-done(((f32[128,64,32]{1,2,0:T(8,128)}), f32[4,64,32]{1,2,0:T(8,128)}) %reduce-scatter.2.cloned.1.call-update) | async-done | bytes 32784 | tf_op jit(solution)/shard_map/reduce_scatter | solution.py:67
  (219 shorter events, 286.4 us)
Async XLA Ops:
  6.5 6.7 %copy-start.1 = (bf16[3,64,4,8,128]{4,3,2,1,0:T(8,128)(2,1)S(1)}, bf16[3,64,4,8,128]{4,3,2,1,0:T(8,128)(2,1)}, u32[]{:S(2)}) copy-start(bf16[3,64,4,8,128]{4,3,2,1,0:T(8,128)(2,1)} %param.5) | copy-start | bytes 4718596
  6.5 6.7 %copy-start.2 = (f32[4,8,128]{2,1,0:T(8,128)S(1)}, f32[4,8,128]{2,1,0:T(8,128)}, u32[]{:S(2)}) copy-start(f32[4,8,128]{2,1,0:T(8,128)} %param.7) | copy-start | bytes 49156
  6.5 46.8 %all-gather.2.cloned.1.call-start = ((), (), s32[]{:S(2)}) async-start(), calls=%async_computation.1 | async-start | bytes 3932160 | tf_op jit(solution)/shard_map/all_gather | solution.py:76
  9.0 518.5 %reduce-scatter.2.cloned.1.call-start = ((), (), s32[]{:S(2)}) async-start(), calls=%async_computation.2 | async-start | bytes 2162688 | tf_op jit(solution)/shard_map/reduce_scatter | solution.py:67
  10.1 5.0 collective-permute-start
  11.9 6.4 %collective-permute-start.1 = (bf16[3,32,1,8,128]{4,1,0,3,2:T(8,128)(2,1)S(1)}, bf16[3,32,1,8,128]{4,1,0,3,2:T(8,128)(2,1)S(1)}, u32[]{:S(2)}, u32[]{:S(2)}) collective-permute-start(bf16[3,32,1,8,128]{4,1,0,3,2:T(8,128)(2,1)S(1)} %get-tuple-element.203), channel_id=1, source_target_pairs={{8,0},{16,8},{24,16},{32,24},{40,32},{48,40},{56,48},{64,56},{72,6... | collective-permute-start | bytes 589832 | tf_op jit(solution)/shard_map/ppermute | solution.py:19
  13.2 5.1 copy-start
Sparse Core Ops, SparseCore 0:
  9.1 44.1 all-gather.1
  434.4 93.0 reduce-scatter.1
where the time goes:
time: 541 us; the launch traced here: 536 us
  local copies, waits for them, and re-layouts  198 us (37%)
  matrix products  186 us (34%)
  waiting for transfers between devices  128 us (24%)
  between operations  13.5 us (2%)
  other arithmetic  6.63 us (1%)
    dot_general x32, local copies, waits for them, and re-layouts, advance(): jnp.einsum('bjc,abkc->ajkc', trial_block, grad_block, preferred_element_t...  121 us
    dot_general x32, matrix products, advance(): jnp.einsum('aic,ajkc->jik', test_block, convected, preferred_element_type...  106 us
    reduce_scatter x1, waiting for transfers between devices, finish(): lax.psum_scatter(partial_value, 'space', scatter_dimension=0, tiled=True)  93.2 us
    dot_general x32, matrix products, advance(): jnp.einsum('bjc,abkc->ajkc', trial_block, grad_block, preferred_element_t...  79.3 us
    squeeze x128, local copies, waits for them, and re-layouts, pick_row(): lax.dynamic_index_in_dim(lax.dynamic_index_in_dim(array, plane, first, Fa...  69.2 us
    all_gather x1, waiting for transfers between devices, shards(): all_modes = lax.all_gather(trial_modes, 'trial', axis=1, tiled=True)  31.8 us
  transfers between devices with their start and end apart: 4, of which 3 were waited for; matrix products, arithmetic and copies ran while one was open for 1% of the time, Pallas kernels for 0%

commit v1 on v0

v1 whole, which is shorter than its diff:
```python
import functools
import math

import jax
import jax.numpy as jnp
from jax import lax
from jax.experimental import pallas as pl
from jax.experimental.pallas import tpu as pltpu
from jax.sharding import PartitionSpec as P

F = jnp.float32
B = jnp.bfloat16
IB = 16


def kernel(w_ref, u0, u1, u2, u3, um, uc, up, out_ref, acc, gs, us, gb):
    step = pl.program_id(0)
    modes = u0.shape[3]
    tests = w_ref.shape[3]
    rows = uc.shape[1]
    lanes = uc.shape[4]
    y0 = 2 * (step % (rows // 2))
    lane = lax.broadcasted_iota(jnp.int32, (modes, lanes), 1)
    for yy in range(2):
        y = y0 + yy
        for a in range(3):
            c = uc[0, y, a].astype(F)
            gx = (up[0, y, a].astype(F) - um[0, y, a].astype(F)) * 0.5
            hi = jnp.where(y < rows - 1, uc[0, jnp.minimum(y + 1, rows - 1), a].astype(F), 0.0)
            lo = jnp.where(y > 0, uc[0, jnp.maximum(y - 1, 0), a].astype(F), 0.0)
            after = jnp.where(lane < lanes - 1, pltpu.roll(c, lanes - 1, 1), 0.0)
            before = jnp.where(lane > 0, pltpu.roll(c, 1, 1), 0.0)
            gs[yy, a, 0] = gx.astype(B)
            gs[yy, a, 1] = ((hi - lo) * 0.5).astype(B)
            gs[yy, a, 2] = ((after - before) * 0.5).astype(B)
    for q, u in enumerate((u0, u1, u2, u3)):
        for b in range(3):
            for yy in range(2):
                us[q * modes:(q + 1) * modes, (b * 2 + yy) * lanes:(b * 2 + yy + 1) * lanes] = u[0, yy, b]

    @pl.when(step == 0)
    def _():
        acc[...] = jnp.zeros_like(acc)

    def block(ib, carry):
        i0 = ib * IB
        for yy in range(2):
            g = [[[gs[yy, a, b, h:h + 16] for h in range(0, modes, 16)] for b in range(3)] for a in range(3)]
            for i in range(IB):
                wb = [jnp.broadcast_to(w_ref[0, yy, a, pl.ds(i0 + i, 1), :], (16, lanes)).astype(B) for a in range(3)]
                for b in range(3):
                    for h in range(modes // 16):
                        value = wb[0] * g[0][b][h] + wb[1] * g[1][b][h] + wb[2] * g[2][b][h]
                        row = i * modes + h * 16
                        gb[row:row + 16, (b * 2 + yy) * lanes:(b * 2 + yy + 1) * lanes] = value
        off = pl.multiple_of(i0 * modes, IB * modes)
        acc[pl.ds(off, IB * modes), :] += lax.dot_general(
            gb[...], us[...], (((1,), (1,)), ((), ())), preferred_element_type=F
        )
        return carry

    lax.fori_loop(0, tests // IB, block, 0)

    @pl.when(step == pl.num_programs(0) - 1)
    def _():
        out_ref[...] = acc[...].T


def compute(w, quarters, padded):
    planes, rows, _, tests, lanes = w.shape
    modes = padded.shape[3]
    pairs = rows // 2
    total = 4 * modes
    one = lambda s: (s // pairs, s % pairs, 0, 0, 0)
    quarter = pl.BlockSpec((1, 2, 3, modes, lanes), one)

    def plane(d):
        return pl.BlockSpec((1, rows, 3, modes, lanes), lambda s: (s // pairs + d, 0, 0, 0, 0))

    return pl.pallas_call(
        kernel,
        out_shape=jax.ShapeDtypeStruct((total, tests * modes), F),
        grid=(planes * pairs,),
        in_specs=[pl.BlockSpec((1, 2, 3, tests, lanes), one)] + [quarter] * 4 + [plane(0), plane(1), plane(2)],
        out_specs=pl.BlockSpec((total, tests * modes), lambda s: (0, 0)),
        scratch_shapes=[
            pltpu.VMEM((tests * modes, total), F),
            pltpu.VMEM((2, 3, 3, modes, lanes), B),
            pltpu.VMEM((total, 6 * lanes), B),
            pltpu.VMEM((IB * modes, 6 * lanes), B),
        ],
    )(w, *quarters, padded, padded, padded)


def exchange(parts, index, pairs, count):
    kept = lax.dynamic_index_in_dim(parts, index(0), 0, False)
    arrived = [
        lax.ppermute(lax.dynamic_index_in_dim(parts, index(d), 0, False).astype(B), "space", pairs(d))
        for d in range(1, count)
    ]
    for value in arrived:
        kept = kept + value.astype(F)
    return kept


def reduce_scatter(partial_value):
    total, width = partial_value.shape
    me = lax.axis_index("space")
    core, z, y = me % 2, (me // 2) % 4, me // 8
    x = lax.axis_index("trial")

    def where(y, z, core):
        return (y * 4 + z) * 2 + core

    every = [(y, z, c) for y in range(4) for z in range(4) for c in range(2)]
    along_core = lambda d: [(where(y, z, c), where(y, z, (c + d) % 2)) for y, z, c in every]
    along_y = lambda d: [(where(y, z, c), where((y + d) % 4, z, c)) for y, z, c in every]
    along_z = lambda d: [(where(y, z, c), where(y, (z + d) % 4, c)) for y, z, c in every]
    parts = partial_value.reshape(4, 4, 2, total // 32 * width // 128, 128).transpose(2, 0, 1, 3, 4)
    parts = exchange(parts, lambda d: (core + d) % 2, along_core, 2)
    parts = exchange(parts, lambda d: (y + d - x) % 4, along_y, 4)
    return exchange(parts, lambda d: (z + d) % 4, along_z, 4)


def shards(test_modes, trial_modes, volumes):
    planes = trial_modes.shape[2]
    modes = trial_modes.shape[1]
    tests = test_modes.shape[1]
    space = lax.axis_size("space")
    cell_count = planes * trial_modes.shape[3] * trial_modes.shape[4]
    factor = 1.0 / (4.0 * math.sqrt(cell_count * space))
    own = trial_modes.transpose(2, 3, 0, 1, 4)
    ring = lambda d: [(i, (i + d) % 4) for i in range(4)]
    left = lax.ppermute(own, "trial", ring(1))
    right = lax.ppermute(own, "trial", ring(-1))
    below = lax.ppermute(own[-1:], "space", [(i, i + 1) for i in range(space - 1)])
    above = lax.ppermute(own[:1], "space", [(i + 1, i) for i in range(space - 1)])
    padded = jnp.concatenate([below, own, above])
    weighted = (test_modes.astype(F) * volumes).transpose(2, 3, 0, 1, 4)
    half = planes // 2
    far = jnp.concatenate(
        [lax.ppermute(left[:half], "trial", ring(1)), lax.ppermute(right[half:], "trial", ring(-1))]
    )
    partial_value = compute(weighted, (own, right, far, left), padded)
    mine = reduce_scatter(partial_value)
    return mine.reshape(-1, tests, modes) * factor


def solution(mesh):
    return jax.shard_map(
        shards,
        mesh=mesh,
        in_specs=(
            P(None, "test", "space", None, None),
            P(None, "trial", "space", None, None),
            P("space", None, None),
        ),
        out_specs=P("space", "test", "trial"),
        check_vma=False,
    )
```

time: 541 us -> 98 us (0.18)
  local copies, waits for them, and re-layouts: 198 us -> 3.83 us
  matrix products: 186 us -> 0 us
  waiting for transfers between devices: 128 us -> 29.1 us
  Pallas kernels: 0 us -> 33.8 us
  starting transfers between devices: 3.09 us -> 23.5 us
  between operations: 13.5 us -> 0.27 us
    dot_general x64 -> x0, matrix products: 186 us -> none  [the longest x32 106 us: advance(): jnp.einsum('aic,ajkc->jik', test_block, convected, preferred_element_type...]
    dot_general x32 -> x0, local copies, waits for them, and re-layouts: 121 us -> none  [advance(): jnp.einsum('bjc,abkc->ajkc', trial_block, grad_block, preferred_element_t...]
    reduce_scatter x1 -> x0, waiting for transfers between devices: 93.2 us -> none  [finish(): lax.psum_scatter(partial_value, 'space', scatter_dimension=0, tiled=True)]
    squeeze x128 -> x0, local copies, waits for them, and re-layouts: 69.2 us -> none  [pick_row(): lax.dynamic_index_in_dim(lax.dynamic_index_in_dim(array, plane, first, Fa...]
    pallas_call x0 -> x1, Pallas kernels: none -> 33.8 us  [compute(): pl.pallas_call(kernel, out_shape=jax.ShapeDtypeStruct((total, tests * mod...]
    all_gather x1 -> x0, waiting for transfers between devices: 31.8 us -> none  [shards(): all_modes = lax.all_gather(trial_modes, 'trial', axis=1, tiled=True)]
    ppermute x2 -> x13, waiting for transfers between devices: 3.19 us -> 29.1 us  [the longest x1 12.6 us: shards(): right = lax.ppermute(own, 'trial', ring(-1))]
    ppermute x2 -> x13, starting transfers between devices: 3.04 us -> 23.5 us  [the longest x7 15 us: exchange(): lax.ppermute(lax.dynamic_index_in_dim(parts, index(d), 0, False).astype(B...]
  transfers between devices with their start and end apart: 4 -> 13, of which waited for: 3 -> 9; matrix products, arithmetic and copies ran while one was open for 1% -> 5% of each run, Pallas kernels for 0% -> 0%
where the time goes in v1:
time: 98 us; the launch traced here: 96.2 us
  Pallas kernels  33.8 us (34%)
  waiting for transfers between devices  29.1 us (30%)
  starting transfers between devices  23.5 us (24%)
  other arithmetic  5.8 us (6%)
  local copies, waits for them, and re-layouts  3.83 us (4%)
    pallas_call x1, Pallas kernels, compute(): pl.pallas_call(kernel, out_shape=jax.ShapeDtypeStruct((total, tests * mod...  33.8 us
    ppermute x7, starting transfers between devices, exchange(): lax.ppermute(lax.dynamic_index_in_dim(parts, index(d), 0, False).astype(B...  15 us
    ppermute x1, waiting for transfers between devices, shards(): right = lax.ppermute(own, 'trial', ring(-1))  12.6 us
    ppermute x7, waiting for transfers between devices, exchange(): lax.ppermute(lax.dynamic_index_in_dim(parts, index(d), 0, False).astype(B...  10.4 us
    transpose x1, other arithmetic, shards(): weighted = (test_modes.astype(F) * volumes).transpose(2, 3, 0, 1, 4)  3.6 us
    ppermute x1, waiting for transfers between devices, shards(): lax.ppermute(right[half:], 'trial', ring(-1))  3.07 us
    ppermute x1, starting transfers between devices, shards(): lax.ppermute(own[-1:], 'space', [(i, i + 1) for i in range(space - 1)])  3.04 us
    ppermute x1, waiting for transfers between devices, shards(): lax.ppermute(left[:half], 'trial', ring(1))  2.6 us
  transfers between devices with their start and end apart: 13, of which 9 were waited for; matrix products, arithmetic and copies ran while one was open for 5% of the time, Pallas kernels for 0%

profile of v1, /device:TPU:2, one launch (start us, length us, event | category | flops | bytes accessed | tf_op | source)
XLA Modules:
  0.0 96.2 jit_solution(9291194411914148017)
XLA Ops:
  0.0 1.4 %copy.13 = bf16[3,32,4,8,128]{4,1,0,3,2:T(8,128)(2,1)S(1)} copy(bf16[3,32,4,8,128]{4,3,2,1,0:T(8,128)(2,1)} %param.4) | data formatting | bytes 1572864 | tf_op args[1]
  1.5 0.0 copy-start.3
  1.5 2.3 %collective-permute-start = (bf16[4,8,3,32,128]{4,3,2,1,0:T(8,128)(2,1)S(1)}, bf16[4,8,3,32,128]{4,3,2,1,0:T(8,128)(2,1)S(1)}, u32[]{:S(2)}, u32[]{:S(2)}) collective-permute-start(bf16[4,8,3,32,128]{4,3,2,1,0:T(8,128)(2,1)S(1)} %bitcast.39), channel_id=1, source_target_pairs={{0,3},{1,0},{2,1},{3,2},{4,7},{5,4},{6,5},{7,6},{8,11},{9,8},{10,9... | collective-permute-start | bytes 2359304 | tf_op jit(solution)/shard_map/ppermute | solution.py:135
  3.8 1.3 %collective-permute-start.5 = (bf16[1,8,3,32,128]{4,3,2,1,0:T(8,128)(2,1)S(1)}, bf16[1,8,3,32,128]{4,3,2,1,0:T(8,128)(2,1)S(1)}, u32[]{:S(2)}, u32[]{:S(2)}) collective-permute-start(bf16[1,8,3,32,128]{4,3,2,1,0:T(8,128)(2,1)S(1)} %get-tuple-element.6), channel_id=1, source_target_pairs={{8,0},{16,8},{24,16},{32,24},{40,32},{48,40},{56,48},{64,56},{72,6... | collective-permute-start | bytes 589832 | tf_op jit(solution)/shard_map/ppermute | solution.py:137
  5.1 3.0 %collective-permute-start.4 = (bf16[1,8,3,32,128]{4,3,2,1,0:T(8,128)(2,1)S(1)}, bf16[1,8,3,32,128]{4,3,2,1,0:T(8,128)(2,1)S(1)}, u32[]{:S(2)}, u32[]{:S(2)}) collective-permute-start(bf16[1,8,3,32,128]{4,3,2,1,0:T(8,128)(2,1)S(1)} %get-tuple-element.5), channel_id=1, source_target_pairs={{0,8},{8,16},{16,24},{24,32},{32,40},{40,48},{48,56},{56,64},{64,7... | collective-permute-start | bytes 589832 | tf_op jit(solution)/shard_map/ppermute | solution.py:136
  8.2 12.6 %collective-permute-done.u1 = bf16[4,8,3,32,128]{4,3,2,1,0:T(8,128)(2,1)S(1)} collective-permute-done((bf16[4,8,3,32,128]{4,3,2,1,0:T(8,128)(2,1)S(1)}, bf16[4,8,3,32,128]{4,3,2,1,0:T(8,128)(2,1)S(1)}, u32[]{:S(2)}, u32[]{:S(2)}) %collective-permute-start) | collective-permute-done | bytes 786464 | tf_op jit(solution)/shard_map/ppermute | solution.py:135
  20.9 0.9 collective-permute-start.3
  21.7 0.3 collective-permute-done.1.u3
  22.1 0.9 collective-permute-start.2
  23.1 3.6 %multiply_bitcast_fusion.w_ref = f32[4,8,3,64,128]{4,3,2,1,0:T(8,128)} fusion(bf16[3,64,4,8,128]{4,3,2,1,0:T(8,128)(2,1)} %param.3, f32[4,8,128]{2,1,0:T(8,128)S(1)} %copy-done.3), kind=kLoop, calls=%fused_computation | loop fusion | flops 1572864 | bytes 4734976 | tf_op jit(solution)/shard_map/transpose | solution.py:139
  26.7 0.0 collective-permute-done.5
  26.7 1.2 %pad_maximum_fusion.um.uc.up = bf16[6,8,3,32,128]{4,3,2,1,0:T(8,128)(2,1)} fusion(bf16[1,8,3,32,128]{4,3,2,1,0:T(8,128)(2,1)S(1)} %collective-permute-done.5, bf16[4,8,3,32,128]{4,3,2,1,0:T(8,128)(2,1)S(1)} %bitcast.42, bf16[1,8,3,32,128]{4,3,2,1,0:T(8,128)(2,1)S(1)} %collective-permute-done.4), kind=kLoop, calls=%fused_computation.1 | loop fusion | flops 1179648 | bytes 2359296 | tf_op jit(solution)/shard_map/concatenate | solution.py:138
  27.9 3.1 %collective-permute-done.3 = bf16[2,8,3,32,128]{4,3,2,1,0:T(8,128)(2,1)S(1)} collective-permute-done((bf16[2,8,3,32,128]{4,3,2,1,0:T(8,128)(2,1)S(1)}, bf16[2,8,3,32,128]{4,3,2,1,0:T(8,128)(2,1)S(1)}, u32[]{:S(2)}, u32[]{:S(2)}) %collective-permute-start.3) | collective-permute-done | bytes 393248 | tf_op jit(solution)/shard_map/ppermute | solution.py:142
  30.9 2.6 %collective-permute-done.2 = bf16[2,8,3,32,128]{4,3,2,1,0:T(8,128)(2,1)S(1)} collective-permute-done((bf16[2,8,3,32,128]{4,3,2,1,0:T(8,128)(2,1)S(1)}, bf16[2,8,3,32,128]{4,3,2,1,0:T(8,128)(2,1)S(1)}, u32[]{:S(2)}, u32[]{:S(2)}) %collective-permute-start.2) | collective-permute-done | bytes 393248 | tf_op jit(solution)/shard_map/ppermute | solution.py:142
  33.5 0.9 pad_maximum_fusion.1.u2
  34.5 33.8 %shard_map.37 = f32[128,2048]{1,0:T(8,128)} custom-call(f32[4,8,3,64,128]{4,3,2,1,0:T(8,128)} %multiply_bitcast_fusion.w_ref, bf16[4,8,3,32,128]{4,3,2,1,0:T(8,128)(2,1)} %bitcast.43, bf16[4,8,3,32,128]{4,3,2,1,0:T(8,128)(2,1)} %copy-done.1, bf16[4,8,3,32,128]{4,3,2,1,0:T(8,128)(2,1)} %pad_maximum_fusion.1.u2, bf16[4,8,3,32,128]{4,3,2,1,0:T(8,128)(2,1)} %copy-done.2, ...), custom_call_target="tpu_custom_call" | custom-call | tf_op jit(solution)/shard_map/pallas_call | solution.py:80
  68.3 1.4 %reshape.18 = f32[4,4,2,64,128]{4,3,2,1,0:T(8,128)S(1)} reshape(f32[128,2048]{1,0:T(8,128)} %shard_map.37) | data formatting | bytes 2097152 | tf_op jit(solution)/shard_map/reshape | solution.py:119
  69.7 0.1 collective-permute-start.6
  69.9 1.4 %collective-permute-done.6 = bf16[4,4,64,128]{3,2,1,0:T(8,128)(2,1)S(1)} collective-permute-done((bf16[4,4,64,128]{3,2,1,0:T(8,128)(2,1)S(1)}, bf16[4,4,64,128]{3,2,1,0:T(8,128)(2,1)S(1)}, u32[]{:S(2)}, u32[]{:S(2)}) %collective-permute-start.6) | collective-permute-done | bytes 262176 | tf_op jit(solution)/shard_map/ppermute | solution.py:98
  71.4 0.1 bitcast_add_fusion
  71.5 3.1 %collective-permute-start.9 = (bf16[4,64,128]{2,1,0:T(8,128)(2,1)S(1)}, bf16[4,64,128]{2,1,0:T(8,128)(2,1)S(1)}, u32[]{:S(2)}, u32[]{:S(2)}) collective-permute-start(bf16[4,64,128]{2,1,0:T(8,128)(2,1)S(1)} %get-tuple-element.8), channel_id=1, source_target_pairs={{0,192},{8,200},{16,208},{24,216},{32,224},{40,232},{48,240},{56,2... | collective-permute-start | bytes 196616 | tf_op jit(solution)/shard_map/ppermute | solution.py:98
  74.6 0.6 collective-permute-start.8
  75.2 1.0 %collective-permute-start.7 = (bf16[4,64,128]{2,1,0:T(8,128)(2,1)S(1)}, bf16[4,64,128]{2,1,0:T(8,128)(2,1)S(1)}, u32[]{:S(2)}, u32[]{:S(2)}) collective-permute-start(bf16[4,64,128]{2,1,0:T(8,128)(2,1)S(1)} %get-tuple-element.7), channel_id=1, source_target_pairs={{0,64},{8,72},{16,80},{24,88},{32,96},{40,104},{48,112},{56,120},{... | collective-permute-start | bytes 196616 | tf_op jit(solution)/shard_map/ppermute | solution.py:98
  76.2 1.5 %collective-permute-done.9 = bf16[4,64,128]{2,1,0:T(8,128)(2,1)S(1)} collective-permute-done((bf16[4,64,128]{2,1,0:T(8,128)(2,1)S(1)}, bf16[4,64,128]{2,1,0:T(8,128)(2,1)S(1)}, u32[]{:S(2)}, u32[]{:S(2)}) %collective-permute-start.9) | collective-permute-done | bytes 65568 | tf_op jit(solution)/shard_map/ppermute | solution.py:98
  77.7 2.9 %collective-permute-done.8 = bf16[4,64,128]{2,1,0:T(8,128)(2,1)S(1)} collective-permute-done((bf16[4,64,128]{2,1,0:T(8,128)(2,1)S(1)}, bf16[4,64,128]{2,1,0:T(8,128)(2,1)S(1)}, u32[]{:S(2)}, u32[]{:S(2)}) %collective-permute-start.8) | collective-permute-done | bytes 65568 | tf_op jit(solution)/shard_map/ppermute | solution.py:98
  80.6 0.7 collective-permute-done.7
  81.4 6.4 %collective-permute-start.12 = (bf16[64,128]{1,0:T(8,128)(2,1)S(1)}, bf16[64,128]{1,0:T(8,128)(2,1)S(1)}, u32[]{:S(2)}, u32[]{:S(2)}) collective-permute-start(bf16[64,128]{1,0:T(8,128)(2,1)S(1)} %get-tuple-element.11), channel_id=1, source_target_pairs={{0,48},{8,56},{16,0},{24,8},{32,16},{40,24},{48,32},{56,40},{64,11... | collective-permute-start | bytes 49160 | tf_op jit(solution)/shard_map/ppermute | solution.py:98
  87.8 1.0 %collective-permute-start.11 = (bf16[64,128]{1,0:T(8,128)(2,1)S(1)}, bf16[64,128]{1,0:T(8,128)(2,1)S(1)}, u32[]{:S(2)}, u32[]{:S(2)}) collective-permute-start(bf16[64,128]{1,0:T(8,128)(2,1)S(1)} %get-tuple-element.12), channel_id=1, source_target_pairs={{0,32},{8,40},{16,48},{24,56},{32,0},{40,8},{48,16},{56,24},{64,96... | collective-permute-start | bytes 49160 | tf_op jit(solution)/shard_map/ppermute | solution.py:98
  88.8 2.8 %collective-permute-start.10 = (bf16[64,128]{1,0:T(8,128)(2,1)S(1)}, bf16[64,128]{1,0:T(8,128)(2,1)S(1)}, u32[]{:S(2)}, u32[]{:S(2)}) collective-permute-start(bf16[64,128]{1,0:T(8,128)(2,1)S(1)} %get-tuple-element.10), channel_id=1, source_target_pairs={{0,16},{8,24},{16,32},{24,40},{32,48},{40,56},{48,0},{56,8},{64,80... | collective-permute-start | bytes 49160 | tf_op jit(solution)/shard_map/ppermute | solution.py:98
  91.6 3.8 %collective-permute-done.11 = bf16[64,128]{1,0:T(8,128)(2,1)S(1)} collective-permute-done((bf16[64,128]{1,0:T(8,128)(2,1)S(1)}, bf16[64,128]{1,0:T(8,128)(2,1)S(1)}, u32[]{:S(2)}, u32[]{:S(2)}) %collective-permute-start.11) | collective-permute-done | bytes 16416 | tf_op jit(solution)/shard_map/ppermute | solution.py:98
  95.4 0.1 mul.21
  95.5 0.7 copy.9
  (19 shorter events, 0.2 us)
Async XLA Ops:
  1.4 25.3 %copy-start = (bf16[3,32,4,8,128]{4,1,0,3,2:T(8,128)(2,1)}, bf16[3,32,4,8,128]{4,1,0,3,2:T(8,128)(2,1)S(1)}, u32[]{:S(2)}) copy-start(bf16[3,32,4,8,128]{4,1,0,3,2:T(8,128)(2,1)S(1)} %copy.13) | copy-start | bytes 2359300
  1.5 21.6 %copy-start.3 = (f32[4,8,128]{2,1,0:T(8,128)S(1)}, f32[4,8,128]{2,1,0:T(8,128)}, u32[]{:S(2)}) copy-start(f32[4,8,128]{2,1,0:T(8,128)} %param.5) | copy-start | bytes 49156
  1.5 19.4 %collective-permute-start = (bf16[4,8,3,32,128]{4,3,2,1,0:T(8,128)(2,1)S(1)}, bf16[4,8,3,32,128]{4,3,2,1,0:T(8,128)(2,1)S(1)}, u32[]{:S(2)}, u32[]{:S(2)}) collective-permute-start(bf16[4,8,3,32,128]{4,3,2,1,0:T(8,128)(2,1)S(1)} %bitcast.39), channel_id=1, source_target_pairs={{0,3},{1,0},{2,1},{3,2},{4,7},{5,4},{6,5},{7,6},{8,11},{9,8},{10,9... | collective-permute-start | bytes 2359304 | tf_op jit(solution)/shard_map/ppermute | solution.py:135
  3.8 18.3 %collective-permute-start.1 = (bf16[4,8,3,32,128]{4,3,2,1,0:T(8,128)(2,1)S(1)}, bf16[4,8,3,32,128]{4,3,2,1,0:T(8,128)(2,1)S(1)}, u32[]{:S(2)}, u32[]{:S(2)}) collective-permute-start(bf16[4,8,3,32,128]{4,3,2,1,0:T(8,128)(2,1)S(1)} %bitcast.40), channel_id=1, source_target_pairs={{0,1},{1,2},{2,3},{3,0},{4,5},{5,6},{6,7},{7,4},{8,9},{9,10},{10,1... | collective-permute-start | bytes 2359304 | tf_op jit(solution)/shard_map/ppermute | solution.py:134
  3.8 22.9 %collective-permute-start.5 = (bf16[1,8,3,32,128]{4,3,2,1,0:T(8,128)(2,1)S(1)}, bf16[1,8,3,32,128]{4,3,2,1,0:T(8,128)(2,1)S(1)}, u32[]{:S(2)}, u32[]{:S(2)}) collective-permute-start(bf16[1,8,3,32,128]{4,3,2,1,0:T(8,128)(2,1)S(1)} %get-tuple-element.6), channel_id=1, source_target_pairs={{8,0},{16,8},{24,16},{32,24},{40,32},{48,40},{56,48},{64,56},{72,6... | collective-permute-start | bytes 589832 | tf_op jit(solution)/shard_map/ppermute | solution.py:137
  5.1 21.6 %collective-permute-start.4 = (bf16[1,8,3,32,128]{4,3,2,1,0:T(8,128)(2,1)S(1)}, bf16[1,8,3,32,128]{4,3,2,1,0:T(8,128)(2,1)S(1)}, u32[]{:S(2)}, u32[]{:S(2)}) collective-permute-start(bf16[1,8,3,32,128]{4,3,2,1,0:T(8,128)(2,1)S(1)} %get-tuple-element.5), channel_id=1, source_target_pairs={{0,8},{8,16},{16,24},{24,32},{32,40},{40,48},{48,56},{56,64},{64,7... | collective-permute-start | bytes 589832 | tf_op jit(solution)/shard_map/ppermute | solution.py:136
  20.8 5.9 %copy-start.1 = (bf16[4,8,3,32,128]{4,3,2,1,0:T(8,128)(2,1)}, bf16[4,8,3,32,128]{4,3,2,1,0:T(8,128)(2,1)S(1)}, u32[]{:S(2)}) copy-start(bf16[4,8,3,32,128]{4,3,2,1,0:T(8,128)(2,1)S(1)} %collective-permute-done.u1) | copy-start | bytes 2359300
  20.9 10.1 %collective-permute-start.3 = (bf16[2,8,3,32,128]{4,3,2,1,0:T(8,128)(2,1)S(1)}, bf16[2,8,3,32,128]{4,3,2,1,0:T(8,128)(2,1)S(1)}, u32[]{:S(2)}, u32[]{:S(2)}) collective-permute-start(bf16[2,8,3,32,128]{4,3,2,1,0:T(8,128)(2,1)S(1)} %slice.17), channel_id=1, source_target_pairs={{0,3},{1,0},{2,1},{3,2},{4,7},{5,4},{6,5},{7,6},{8,11},{9,8},{10,9... | collective-permute-start | bytes 1179656 | tf_op jit(solution)/shard_map/ppermute | solution.py:142
  22.1 4.6 %copy-start.2 = (bf16[4,8,3,32,128]{4,3,2,1,0:T(8,128)(2,1)}, bf16[4,8,3,32,128]{4,3,2,1,0:T(8,128)(2,1)S(1)}, u32[]{:S(2)}) copy-start(bf16[4,8,3,32,128]{4,3,2,1,0:T(8,128)(2,1)S(1)} %collective-permute-done.1.u3) | copy-start | bytes 2359300
  22.1 11.4 %collective-permute-start.2 = (bf16[2,8,3,32,128]{4,3,2,1,0:T(8,128)(2,1)S(1)}, bf16[2,8,3,32,128]{4,3,2,1,0:T(8,128)(2,1)S(1)}, u32[]{:S(2)}, u32[]{:S(2)}) collective-permute-start(bf16[2,8,3,32,128]{4,3,2,1,0:T(8,128)(2,1)S(1)} %slice.16), channel_id=1, source_target_pairs={{0,1},{1,2},{2,3},{3,0},{4,5},{5,6},{6,7},{7,4},{8,9},{9,10},{10,1... | collective-permute-start | bytes 1179656 | tf_op jit(solution)/shard_map/ppermute | solution.py:142
  69.7 1.6 %collective-permute-start.6 = (bf16[4,4,64,128]{3,2,1,0:T(8,128)(2,1)S(1)}, bf16[4,4,64,128]{3,2,1,0:T(8,128)(2,1)S(1)}, u32[]{:S(2)}, u32[]{:S(2)}) collective-permute-start(bf16[4,4,64,128]{3,2,1,0:T(8,128)(2,1)S(1)} %fusion), channel_id=1, source_target_pairs={{0,8},{8,0},{16,24},{24,16},{32,40},{40,32},{48,56},{56,48},{64,72... | collective-permute-start | bytes 786440 | tf_op jit(solution)/shard_map/ppermute | solution.py:98
  71.5 6.2 %collective-permute-start.9 = (bf16[4,64,128]{2,1,0:T(8,128)(2,1)S(1)}, bf16[4,64,128]{2,1,0:T(8,128)(2,1)S(1)}, u32[]{:S(2)}, u32[]{:S(2)}) collective-permute-start(bf16[4,64,128]{2,1,0:T(8,128)(2,1)S(1)} %get-tuple-element.8), channel_id=1, source_target_pairs={{0,192},{8,200},{16,208},{24,216},{32,224},{40,232},{48,240},{56,2... | collective-permute-start | bytes 196616 | tf_op jit(solution)/shard_map/ppermute | solution.py:98
  74.6 6.1 %collective-permute-start.8 = (bf16[4,64,128]{2,1,0:T(8,128)(2,1)S(1)}, bf16[4,64,128]{2,1,0:T(8,128)(2,1)S(1)}, u32[]{:S(2)}, u32[]{:S(2)}) collective-permute-start(bf16[4,64,128]{2,1,0:T(8,128)(2,1)S(1)} %get-tuple-element.9), channel_id=1, source_target_pairs={{0,128},{8,136},{16,144},{24,152},{32,160},{40,168},{48,176},{56,1... | collective-permute-start | bytes 196616 | tf_op jit(solution)/shard_map/ppermute | solution.py:98
  75.2 6.1 %collective-permute-start.7 = (bf16[4,64,128]{2,1,0:T(8,128)(2,1)S(1)}, bf16[4,64,128]{2,1,0:T(8,128)(2,1)S(1)}, u32[]{:S(2)}, u32[]{:S(2)}) collective-permute-start(bf16[4,64,128]{2,1,0:T(8,128)(2,1)S(1)} %get-tuple-element.7), channel_id=1, source_target_pairs={{0,64},{8,72},{16,80},{24,88},{32,96},{40,104},{48,112},{56,120},{... | collective-permute-start | bytes 196616 | tf_op jit(solution)/shard_map/ppermute | solution.py:98
  81.4 10.2 %collective-permute-start.12 = (bf16[64,128]{1,0:T(8,128)(2,1)S(1)}, bf16[64,128]{1,0:T(8,128)(2,1)S(1)}, u32[]{:S(2)}, u32[]{:S(2)}) collective-permute-start(bf16[64,128]{1,0:T(8,128)(2,1)S(1)} %get-tuple-element.11), channel_id=1, source_target_pairs={{0,48},{8,56},{16,0},{24,8},{32,16},{40,24},{48,32},{56,40},{64,11... | collective-permute-start | bytes 49160 | tf_op jit(solution)/shard_map/ppermute | solution.py:98
  87.8 7.6 %collective-permute-start.11 = (bf16[64,128]{1,0:T(8,128)(2,1)S(1)}, bf16[64,128]{1,0:T(8,128)(2,1)S(1)}, u32[]{:S(2)}, u32[]{:S(2)}) collective-permute-start(bf16[64,128]{1,0:T(8,128)(2,1)S(1)} %get-tuple-element.12), channel_id=1, source_target_pairs={{0,32},{8,40},{16,48},{24,56},{32,0},{40,8},{48,16},{56,24},{64,96... | collective-permute-start | bytes 49160 | tf_op jit(solution)/shard_map/ppermute | solution.py:98
  88.8 6.7 %collective-permute-start.10 = (bf16[64,128]{1,0:T(8,128)(2,1)S(1)}, bf16[64,128]{1,0:T(8,128)(2,1)S(1)}, u32[]{:S(2)}, u32[]{:S(2)}) collective-permute-start(bf16[64,128]{1,0:T(8,128)(2,1)S(1)} %get-tuple-element.10), channel_id=1, source_target_pairs={{0,16},{8,24},{16,32},{24,40},{32,48},{40,56},{48,0},{56,8},{64,80... | collective-permute-start | bytes 49160 | tf_op jit(solution)/shard_map/ppermute | solution.py:98
